TPU v7x, 256 devices: a whole 4x4x8 slice. The times are simulated.
256 devices in a mesh: dp: 8 (over z), seq: 32 (over x, y, core).
Axes of the slice: x: 4, y: 4, z: 8, core: 2. Of those that a mesh axis runs over, the one named last changes fastest.
Arguments:
- tokens: bfloat16 [8, 16384, 256], P('dp', 'seq'), may hold values from -6 to 6
- cotangent: bfloat16 [8, 16384, 256], P('dp', 'seq'), may hold values from -6 to 6
- w_in: bfloat16 [256, 768], replicated, may hold values from -0.375 to 0.375
- w_out: bfloat16 [256, 256], replicated, may hold values from -0.375 to 0.375
- filter_taps: float32 [16384, 256], P('seq'), may hold values from -0.046875 to 0.046875
- skip: float32 [256], replicated, may hold values from -4 to 4
Outputs:
- output: bfloat16 [8, 16384, 256], P('dp', 'seq')
- dinput: bfloat16 [8, 16384, 256], P('dp', 'seq')
- grad_in_proj: float32 [256, 768], P('dp')
- grad_out_proj: float32 [256, 256], P('dp')
- grad_filter: float32 [16384, 256], P('seq', 'dp')
- grad_skip: float32 [256], P('dp')
All inputs are finite; a program needn't handle non-finite values.
Results may differ from a plain program's by a relative error of at most 0.0049.
Values sent between devices are 32-bit elements; how exact they have to be, the bound alone decides.
A program may use at most 128 MiB of HBM per device.

v0:
```python
import math
import jax
import jax.numpy as jnp
from jax import lax
from jax.sharding import PartitionSpec as P

HIGHEST = lax.Precision.HIGHEST


def regroup_real(signal):
    return lax.all_to_all(signal, "seq", split_axis=1, concat_axis=0, tiled=True)


def regroup_spectral(signal):
    return lax.all_to_all(signal, "seq", split_axis=1, concat_axis=0, tiled=True)


def angles(first_index, second_index, modulus):
    product = first_index[:, None] * second_index[None, :] % modulus
    return 2.0 * math.pi / modulus * product.astype(jnp.float32)


def forward_spectrum(signal):
    tok_rows, chan_count = signal.shape
    seq_parts = lax.axis_size("seq")
    block_rows = tok_rows // seq_parts
    full_length = 2 * seq_parts * tok_rows
    seq_index = lax.axis_index("seq")
    regrouped = regroup_real(signal[None])
    freq_index = jnp.arange(2 * seq_parts, dtype=jnp.int32)
    slot_index = jnp.arange(seq_parts, dtype=jnp.int32)
    outer_angle = angles(freq_index, slot_index, 2 * seq_parts)
    first_re = jnp.einsum("ks,scf->ckf", jnp.cos(outer_angle), regrouped, precision=HIGHEST)
    first_im = jnp.einsum("ks,scf->ckf", -jnp.sin(outer_angle), regrouped, precision=HIGHEST)
    local_pos = seq_index * block_rows + jnp.arange(block_rows, dtype=jnp.int32)
    twiddle = angles(local_pos, freq_index, full_length)[:, :, None]
    tw_cos = jnp.cos(twiddle)
    tw_sin = -jnp.sin(twiddle)
    packed = jnp.concatenate(
        [first_re * tw_cos - first_im * tw_sin, first_re * tw_sin + first_im * tw_cos], axis=2
    )
    spread = regroup_spectral(packed)
    row_index = jnp.arange(tok_rows, dtype=jnp.int32)
    inner_angle = angles(row_index, row_index, tok_rows)
    cos_part = jnp.einsum("kc,cjf->kjf", jnp.cos(inner_angle), spread, precision=HIGHEST)
    sin_part = jnp.einsum("kc,cjf->kjf", -jnp.sin(inner_angle), spread, precision=HIGHEST)
    spectrum = jnp.concatenate(
        [
            cos_part[..., :chan_count] - sin_part[..., chan_count:],
            sin_part[..., :chan_count] + cos_part[..., chan_count:],
        ],
        axis=2,
    )
    spectrum = lax.all_to_all(spectrum, "seq", split_axis=0, concat_axis=1, tiled=True)
    return spectrum


def inverse_field(spectrum):
    spectrum = lax.all_to_all(spectrum, "seq", split_axis=1, concat_axis=0, tiled=True)
    tok_rows = spectrum.shape[0]
    chan_count = spectrum.shape[2] // 2
    seq_parts = lax.axis_size("seq")
    block_rows = tok_rows // seq_parts
    full_length = 2 * seq_parts * tok_rows
    seq_index = lax.axis_index("seq")
    row_index = jnp.arange(tok_rows, dtype=jnp.int32)
    inner_angle = angles(row_index, row_index, tok_rows)
    cos_part = jnp.einsum("kc,kjf->jcf", jnp.cos(inner_angle), spectrum, precision=HIGHEST)
    sin_part = jnp.einsum("kc,kjf->jcf", jnp.sin(inner_angle), spectrum, precision=HIGHEST)
    packed = jnp.concatenate(
        [
            cos_part[..., :chan_count] - sin_part[..., chan_count:],
            sin_part[..., :chan_count] + cos_part[..., chan_count:],
        ],
        axis=2,
    )
    regrouped = regroup_spectral(packed)
    freq_index = jnp.arange(2 * seq_parts, dtype=jnp.int32)
    slot_index = jnp.arange(seq_parts, dtype=jnp.int32)
    local_pos = seq_index * block_rows + jnp.arange(block_rows, dtype=jnp.int32)
    twiddle = angles(freq_index, local_pos, full_length)[:, :, None]
    tw_cos = jnp.cos(twiddle)
    tw_sin = jnp.sin(twiddle)
    moved_re = regrouped[..., :chan_count]
    moved_im = regrouped[..., chan_count:]
    turned_re = moved_re * tw_cos - moved_im * tw_sin
    turned_im = moved_re * tw_sin + moved_im * tw_cos
    outer_angle = angles(slot_index, freq_index, 2 * seq_parts)
    outer_cos = jnp.cos(outer_angle)
    outer_sin = jnp.sin(outer_angle)
    signal = jnp.einsum("sk,kcf->csf", outer_cos, turned_re, precision=HIGHEST) - jnp.einsum(
        "sk,kcf->csf", outer_sin, turned_im, precision=HIGHEST
    )
    signal = signal * (1.0 / full_length)
    return regroup_real(signal)[:, 0, :]


def invert_real(real_part, imag_part):
    return inverse_field(jnp.concatenate([real_part, imag_part], axis=2))


def shards(tokens, cotangent, w_in, w_out, filter_taps, skip):
    model_width = w_out.shape[0]
    seq_in = tokens[0]
    grad_out = cotangent[0]
    projected = jnp.dot(seq_in, w_in, preferred_element_type=jnp.float32)
    gate_out = projected[:, :model_width]
    gate_in = projected[:, model_width : 2 * model_width]
    values = projected[:, 2 * model_width :]
    gated = values * gate_in
    joint_spec = forward_spectrum(jnp.concatenate([gated, filter_taps], axis=1))
    gated_re = joint_spec[..., :model_width]
    taps_re = joint_spec[..., model_width : 2 * model_width]
    gated_im = joint_spec[..., 2 * model_width : 3 * model_width]
    taps_im = joint_spec[..., 3 * model_width :]
    prod_re = taps_re * gated_re - taps_im * gated_im
    prod_im = taps_re * gated_im + taps_im * gated_re
    conv = invert_real(prod_re, prod_im) + skip * gated
    mixed = (conv * gate_out).astype(jnp.bfloat16)
    output = jnp.dot(mixed, w_out, preferred_element_type=jnp.float32).astype(jnp.bfloat16)
    dmixed = lax.dot_general(
        grad_out, w_out, (((1,), (1,)), ((), ())), preferred_element_type=jnp.float32
    )
    dconv = dmixed * gate_out
    dconv_spec = forward_spectrum(dconv)
    dconv_re = dconv_spec[..., :model_width]
    dconv_im = dconv_spec[..., model_width:]
    taps_corr_re = taps_re * dconv_re + taps_im * dconv_im
    taps_corr_im = taps_re * dconv_im - taps_im * dconv_re
    gated_corr_re = gated_re * dconv_re + gated_im * dconv_im
    gated_corr_im = gated_re * dconv_im - gated_im * dconv_re
    back_field = invert_real(
        jnp.concatenate([taps_corr_re, gated_corr_re], axis=2),
        jnp.concatenate([taps_corr_im, gated_corr_im], axis=2),
    )
    dgated = back_field[:, :model_width] + skip * dconv
    taps_term = back_field[:, model_width:]
    dproj = jnp.concatenate([dmixed * conv, dgated * values, dgated * gate_in], axis=1).astype(
        jnp.bfloat16
    )
    dinput = lax.dot_general(
        dproj, w_in, (((1,), (1,)), ((), ())), preferred_element_type=jnp.float32
    ).astype(jnp.bfloat16)
    token_total = lax.axis_size("dp") * tokens.shape[0] * lax.axis_size("seq") * tokens.shape[1]
    grad_scale = 1.0 / math.sqrt(token_total)
    in_term = (
        lax.dot_general(seq_in, dproj, (((0,), (0,)), ((), ())), preferred_element_type=jnp.float32)
        * grad_scale
    )
    out_term = (
        lax.dot_general(
            mixed, grad_out, (((0,), (0,)), ((), ())), preferred_element_type=jnp.float32
        )
        * grad_scale
    )
    skip_term = jnp.sum(dconv * gated, axis=0) * grad_scale
    taps_term = taps_term * grad_scale
    in_sum, out_sum, skip_sum = lax.psum((in_term, out_term, skip_term), "seq")
    in_part, out_part, skip_part, taps_part = (
        lax.psum_scatter(in_sum, "dp", scatter_dimension=0, tiled=True),
        lax.psum_scatter(out_sum, "dp", scatter_dimension=0, tiled=True),
        lax.psum_scatter(skip_sum, "dp", scatter_dimension=0, tiled=True),
        lax.psum_scatter(taps_term, "dp", scatter_dimension=1, tiled=True),
    )
    return (output[None], dinput[None], in_part, out_part, taps_part, skip_part)


def solution(mesh):
    return jax.shard_map(
        shards,
        mesh=mesh,
        in_specs=(P("dp", "seq", None), P("dp", "seq", None), P(), P(), P("seq", None), P()),
        out_specs=(
            P("dp", "seq", None),
            P("dp", "seq", None),
            P("dp", None),
            P("dp", None),
            P("seq", "dp"),
            P("dp"),
        ),
        check_vma=False,
    )
```

profile of v0, /device:TPU:2, one launch (start us, length us, event | category | flops | bytes accessed | tf_op | source)
XLA Modules:
  0.0 735.4 jit_solution(1351603968979599347)
XLA Ops:
  13.4 7.7 %all-to-all-start = ((f32[1,512,512]{2,0,1:T(1,128)}), f32[1,512,512]{2,0,1:T(1,128)}, u32[]{:S(2)}, u32[]{:S(2)}) async-start(f32[1,512,512]{2,0,1:T(1,128)} %copy.107), calls=%async_computation | async-start | bytes 2097152 | tf_op jit(solution)/shard_map/all_to_all | solution.py:11
  22.5 13.0 %all-to-all-done = f32[1,512,512]{2,0,1:T(1,128)} async-done(((f32[1,512,512]{2,0,1:T(1,128)}), f32[1,512,512]{2,0,1:T(1,128)}, u32[]{:S(2)}, u32[]{:S(2)}) %all-to-all-start) | async-done | bytes 1048608 | tf_op jit(solution)/shard_map/all_to_all | solution.py:11
  54.0 7.4 %all-to-all-start.1 = ((f32[16,64,1024]{2,0,1:T(8,128)}), f32[16,64,1024]{2,0,1:T(8,128)}, u32[]{:S(2)}, u32[]{:S(2)}) async-start(f32[16,64,1024]{2,0,1:T(8,128)} %copy.110), calls=%async_computation.1 | async-start | bytes 8388608 | tf_op jit(solution)/shard_map/all_to_all | solution.py:15
  67.5 44.2 %all-to-all-done.1 = f32[16,64,1024]{2,0,1:T(8,128)} async-done(((f32[16,64,1024]{2,0,1:T(8,128)}), f32[16,64,1024]{2,0,1:T(8,128)}, u32[]{:S(2)}, u32[]{:S(2)}) %all-to-all-start.1) | async-done | bytes 4194336 | tf_op jit(solution)/shard_map/all_to_all | solution.py:15
  111.7 9.1 %all-to-all-start.7 = ((f32[16,64,512]{2,0,1:T(8,128)}), f32[16,64,512]{2,0,1:T(8,128)}, u32[]{:S(2)}, u32[]{:S(2)}) async-start(f32[16,64,512]{2,0,1:T(8,128)} %copy.127), calls=%async_computation.7 | async-start | bytes 4194304 | tf_op jit(solution)/shard_map/all_to_all | solution.py:15
  123.4 10.9 %fusion.25 = f32[512,2,1024]{2,0,1:T(8,128)S(1)} fusion(f32[512,2,1024]{2,0,1:T(8,128)S(1)} %bitcast.153), kind=kOutput, calls=%fused_computation.52 | convolution fusion | flops 6446383104 | bytes 8388608 | tf_op jit(solution)/shard_map/kc,cjf->kjf/dot_general | solution.py:46
  134.3 19.6 %fusion.31 = f32[512,2,1024]{2,0,1:T(8,128)S(1)} fusion(f32[512,2,1024]{2,0,1:T(8,128)S(1)} %bitcast.154), kind=kOutput, calls=%fused_computation.58 | convolution fusion | flops 6446120960 | bytes 8388608 | tf_op jit(solution)/shard_map/kc,cjf->kjf/dot_general | solution.py:45
  161.0 7.4 %all-to-all-start.2 = ((f32[512,2,1024]{2,1,0:T(2,128)}), f32[512,2,1024]{2,1,0:T(2,128)}, u32[]{:S(2)}, u32[]{:S(2)}) async-start(f32[512,2,1024]{2,1,0:T(2,128)} %copy.112), calls=%async_computation.2 | async-start | bytes 8388608 | tf_op jit(solution)/shard_map/all_to_all | solution.py:54
  170.3 10.7 %fusion.23 = f32[512,2,512]{0,2,1:T(8,128)S(1)} fusion(f32[512,2,512]{2,0,1:T(8,128)S(1)} %bitcast.170), kind=kOutput, calls=%fused_computation.50 | convolution fusion | flops 3225157632 | bytes 4194304 | tf_op jit(solution)/shard_map/kc,cjf->kjf/dot_general | solution.py:46
  180.9 10.6 %fusion.28 = f32[512,2,512]{0,2,1:T(8,128)S(1)} fusion(f32[512,2,512]{2,0,1:T(8,128)S(1)} %bitcast.171), kind=kOutput, calls=%fused_computation.55 | convolution fusion | flops 3224895488 | bytes 4194304 | tf_op jit(solution)/shard_map/kc,cjf->kjf/dot_general | solution.py:45
  197.7 20.9 %all-to-all-done.2 = f32[512,2,1024]{2,1,0:T(2,128)} async-done(((f32[512,2,1024]{2,1,0:T(2,128)}), f32[512,2,1024]{2,1,0:T(2,128)}, u32[]{:S(2)}, u32[]{:S(2)}) %all-to-all-start.2) | async-done | bytes 4194336 | tf_op jit(solution)/shard_map/all_to_all | solution.py:54
  218.7 9.1 %all-to-all-start.8 = ((f32[512,2,512]{2,1,0:T(2,128)}), f32[512,2,512]{2,1,0:T(2,128)}, u32[]{:S(2)}, u32[]{:S(2)}) async-start(f32[512,2,512]{2,1,0:T(2,128)} %copy.131), calls=%async_computation.8 | async-start | bytes 4194304 | tf_op jit(solution)/shard_map/all_to_all | solution.py:54
  235.6 18.1 %all-to-all-done.8 = f32[512,2,512]{2,1,0:T(2,128)} async-done(((f32[512,2,512]{2,1,0:T(2,128)}), f32[512,2,512]{2,1,0:T(2,128)}, u32[]{:S(2)}, u32[]{:S(2)}) %all-to-all-start.8) | async-done | bytes 2097184 | tf_op jit(solution)/shard_map/all_to_all | solution.py:54
  253.8 7.6 %all-to-all-start.3 = ((f32[16,64,512]{2,0,1:T(8,128)}), f32[16,64,512]{2,0,1:T(8,128)}, u32[]{:S(2)}, u32[]{:S(2)}) async-start(f32[16,64,512]{2,0,1:T(8,128)} %pad_maximum_fusion.4), calls=%async_computation.3 | async-start | bytes 4194304 | tf_op jit(solution)/shard_map/all_to_all | solution.py:59
  268.9 18.5 %all-to-all-done.3 = f32[16,64,512]{2,0,1:T(8,128)} async-done(((f32[16,64,512]{2,0,1:T(8,128)}), f32[16,64,512]{2,0,1:T(8,128)}, u32[]{:S(2)}, u32[]{:S(2)}) %all-to-all-start.3) | async-done | bytes 2097184 | tf_op jit(solution)/shard_map/all_to_all | solution.py:59
  287.4 7.7 %all-to-all-start.9 = ((f32[16,64,1024]{2,0,1:T(8,128)}), f32[16,64,1024]{2,0,1:T(8,128)}, u32[]{:S(2)}, u32[]{:S(2)}) async-start(f32[16,64,1024]{2,0,1:T(8,128)} %pad_maximum_fusion.2), calls=%async_computation.9 | async-start | bytes 8388608 | tf_op jit(solution)/shard_map/all_to_all | solution.py:59
  297.0 11.0 %convolution_bitcast_fusion.2 = f32[2,512,512]{1,2,0:T(8,128)S(1)} fusion(f32[512,2,512]{2,0,1:T(8,128)S(1)} %bitcast.172), kind=kOutput, calls=%fused_computation.22 | convolution fusion | flops 3224895488 | bytes 4194304 | tf_op jit(solution)/shard_map/kc,kjf->jcf/dot_general | solution.py:69
  308.0 11.0 %convolution_bitcast_fusion.3 = f32[2,512,512]{1,2,0:T(8,128)S(1)} fusion(f32[512,2,512]{2,0,1:T(8,128)S(1)} %bitcast.173), kind=kOutput, calls=%fused_computation.23 | convolution fusion | flops 3224895488 | bytes 4194304 | tf_op jit(solution)/shard_map/kc,kjf->jcf/dot_general | solution.py:68
  325.2 20.0 %all-to-all-done.9 = f32[16,64,1024]{2,0,1:T(8,128)} async-done(((f32[16,64,1024]{2,0,1:T(8,128)}), f32[16,64,1024]{2,0,1:T(8,128)}, u32[]{:S(2)}, u32[]{:S(2)}) %all-to-all-start.9) | async-done | bytes 4194336 | tf_op jit(solution)/shard_map/all_to_all | solution.py:59
  345.2 9.7 %all-to-all-start.4 = ((f32[2,512,512]{2,0,1:T(2,128)}), f32[2,512,512]{2,0,1:T(2,128)}, u32[]{:S(2)}, u32[]{:S(2)}) async-start(f32[2,512,512]{2,0,1:T(2,128)} %copy.118), calls=%async_computation.4 | async-start | bytes 4194304 | tf_op jit(solution)/shard_map/all_to_all | solution.py:15
  357.5 11.1 %convolution_bitcast_fusion = f32[2,512,1024]{1,2,0:T(8,128)S(1)} fusion(f32[512,2,1024]{2,0,1:T(8,128)S(1)} %bitcast.155), kind=kOutput, calls=%fused_computation.4 | convolution fusion | flops 6446120960 | bytes 8388608 | tf_op jit(solution)/shard_map/kc,kjf->jcf/dot_general | solution.py:69
  368.6 11.3 %convolution_bitcast_fusion.1 = f32[2,512,1024]{1,2,0:T(8,128)S(1)} fusion(f32[512,2,1024]{2,0,1:T(8,128)S(1)} %bitcast.156), kind=kOutput, calls=%fused_computation.5 | convolution fusion | flops 6446120960 | bytes 8388608 | tf_op jit(solution)/shard_map/kc,kjf->jcf/dot_general | solution.py:68
  390.8 7.6 %all-to-all-start.10 = ((f32[2,512,1024]{2,0,1:T(2,128)}), f32[2,512,1024]{2,0,1:T(2,128)}, u32[]{:S(2)}, u32[]{:S(2)}) async-start(f32[2,512,1024]{2,0,1:T(2,128)} %copy.137), calls=%async_computation.10 | async-start | bytes 8388608 | tf_op jit(solution)/shard_map/all_to_all | solution.py:15
  405.1 43.6 %all-to-all-done.10 = f32[2,512,1024]{2,0,1:T(2,128)} async-done(((f32[2,512,1024]{2,0,1:T(2,128)}), f32[2,512,1024]{2,0,1:T(2,128)}, u32[]{:S(2)}, u32[]{:S(2)}) %all-to-all-start.10) | async-done | bytes 4194336 | tf_op jit(solution)/shard_map/all_to_all | solution.py:15
  448.6 9.1 %all-to-all-start.5 = ((f32[16,32,256]{2,0,1:T(8,128)}), f32[16,32,256]{2,0,1:T(8,128)S(1)}, u32[]{:S(2)}, u32[]{:S(2)}) async-start(f32[16,32,256]{2,0,1:T(8,128)} %copy.123), calls=%async_computation.5 | async-start | bytes 1048576 | tf_op jit(solution)/shard_map/all_to_all | solution.py:11
  469.4 21.9 %all_to_all.198 = f32[16,32,512]{2,0,1:T(8,128)S(1)} all-to-all(f32[16,32,512]{2,0,1:T(8,128)} %copy.142), channel_id=1, replica_groups=mesh['dp'=8,'seq'=32] {'seq'}, dimensions={1} | all-to-all | bytes 2097152 | tf_op jit(solution)/shard_map/all_to_all | solution.py:11
  497.3 38.6 %reduce-scatter.12.cloned.1.call-done = f32[32,768]{1,0:T(8,128)} async-done(((f32[256,768]{1,0:T(8,128)}), f32[32,768]{1,0:T(8,128)}) %reduce-scatter.12.cloned.1.call-update) | async-done | bytes 98320
  540.0 15.6 %all-reduce = f32[256]{0:T(256)S(1)} all-reduce(f32[256]{0:T(256)S(1)} %broadcast_multiply_fusion), channel_id=5, replica_groups=mesh['dp'=8,'seq'=32] {'dp'}, use_global_device_ids=true, to_apply=%region_7.8.clone | all-reduce | flops 256 | bytes 2048
  557.7 16.3 %reduce-scatter.8.cloned.1.call-done = f32[32,256]{1,0:T(8,128)} async-done(((f32[256,256]{1,0:T(8,128)}), f32[32,256]{1,0:T(8,128)}) %reduce-scatter.8.cloned.1.call-update) | async-done | bytes 32784 | tf_op jit(solution)/shard_map/reduce_scatter | solution.py:161
  574.0 106.2 %all-reduce.1 = (f32[32,256]{1,0:T(8,128)}, f32[32]{0:T(128)}) all-reduce(f32[32,256]{1,0:T(8,128)} %reduce-scatter.8.cloned.1.call-done, f32[32]{0:T(128)S(1)} %dynamic-slice.1), channel_id=1, replica_groups=mesh['dp'=8,'seq'=32] {'seq'}, use_global_device_ids=true, to_apply=%region_2.3 | all-reduce | flops 8224 | bytes 65792 | tf_op jit(solution)/shard_map/psum | solution.py:158
  680.2 8.0 %all-reduce.4.cloned.1.call-done = f32[32,768]{0,1:T(8,128)} async-done(((f32[32,768]{0,1:T(8,128)}), f32[32,768]{0,1:T(8,128)}) %all-reduce.4.cloned.1.call-update) | async-done | bytes 98320 | tf_op jit(solution)/shard_map/psum | solution.py:158
  690.0 38.5 %reduce-scatter.10.cloned.1.call-done = f32[32,512]{1,0:T(8,128)} async-done(((f32[256,512]{1,0:T(8,128)}), f32[32,512]{1,0:T(8,128)}) %reduce-scatter.10.cloned.1.call-update) | async-done | bytes 65552
  (129 shorter events, 117.7 us)
Async XLA Ops:
  7.2 2.3 copy-start.6
  7.2 2.3 copy-start.8
  7.2 3.9 copy-start.10
  13.4 22.2 %all-to-all-start = ((f32[1,512,512]{2,0,1:T(1,128)}), f32[1,512,512]{2,0,1:T(1,128)}, u32[]{:S(2)}, u32[]{:S(2)}) async-start(f32[1,512,512]{2,0,1:T(1,128)} %copy.107), calls=%async_computation | async-start | bytes 2097152 | tf_op jit(solution)/shard_map/all_to_all | solution.py:11
  22.4 13.1 %copy-start.21 = (s32[16]{0:T(128)}, s32[16]{0:T(128)S(1)}, u32[]{:S(2)}) copy-start(s32[16]{0:T(128)S(1)} %iota_add_fusion) | copy-start | bytes 196
  35.5 18.5 %all-to-all-start.6 = ((f32[1,512,256]{2,0,1:T(1,128)}), f32[1,512,256]{2,0,1:T(1,128)S(1)}, u32[]{:S(2)}, u32[]{:S(2)}) async-start(f32[1,512,256]{2,0,1:T(1,128)} %copy.124), calls=%async_computation.6 | async-start | bytes 1048576 | tf_op jit(solution)/shard_map/all_to_all | solution.py:11
  54.0 57.7 %all-to-all-start.1 = ((f32[16,64,1024]{2,0,1:T(8,128)}), f32[16,64,1024]{2,0,1:T(8,128)}, u32[]{:S(2)}, u32[]{:S(2)}) async-start(f32[16,64,1024]{2,0,1:T(8,128)} %copy.110), calls=%async_computation.1 | async-start | bytes 8388608 | tf_op jit(solution)/shard_map/all_to_all | solution.py:15
  111.7 49.2 %all-to-all-start.7 = ((f32[16,64,512]{2,0,1:T(8,128)}), f32[16,64,512]{2,0,1:T(8,128)}, u32[]{:S(2)}, u32[]{:S(2)}) async-start(f32[16,64,512]{2,0,1:T(8,128)} %copy.127), calls=%async_computation.7 | async-start | bytes 4194304 | tf_op jit(solution)/shard_map/all_to_all | solution.py:15
  161.0 57.7 %all-to-all-start.2 = ((f32[512,2,1024]{2,1,0:T(2,128)}), f32[512,2,1024]{2,1,0:T(2,128)}, u32[]{:S(2)}, u32[]{:S(2)}) async-start(f32[512,2,1024]{2,1,0:T(2,128)} %copy.112), calls=%async_computation.2 | async-start | bytes 8388608 | tf_op jit(solution)/shard_map/all_to_all | solution.py:54
  218.7 35.1 %all-to-all-start.8 = ((f32[512,2,512]{2,1,0:T(2,128)}), f32[512,2,512]{2,1,0:T(2,128)}, u32[]{:S(2)}, u32[]{:S(2)}) async-start(f32[512,2,512]{2,1,0:T(2,128)} %copy.131), calls=%async_computation.8 | async-start | bytes 4194304 | tf_op jit(solution)/shard_map/all_to_all | solution.py:54
  253.8 33.6 %all-to-all-start.3 = ((f32[16,64,512]{2,0,1:T(8,128)}), f32[16,64,512]{2,0,1:T(8,128)}, u32[]{:S(2)}, u32[]{:S(2)}) async-start(f32[16,64,512]{2,0,1:T(8,128)} %pad_maximum_fusion.4), calls=%async_computation.3 | async-start | bytes 4194304 | tf_op jit(solution)/shard_map/all_to_all | solution.py:59
  287.4 57.8 %all-to-all-start.9 = ((f32[16,64,1024]{2,0,1:T(8,128)}), f32[16,64,1024]{2,0,1:T(8,128)}, u32[]{:S(2)}, u32[]{:S(2)}) async-start(f32[16,64,1024]{2,0,1:T(8,128)} %pad_maximum_fusion.2), calls=%async_computation.9 | async-start | bytes 8388608 | tf_op jit(solution)/shard_map/all_to_all | solution.py:59
  345.2 45.5 %all-to-all-start.4 = ((f32[2,512,512]{2,0,1:T(2,128)}), f32[2,512,512]{2,0,1:T(2,128)}, u32[]{:S(2)}, u32[]{:S(2)}) async-start(f32[2,512,512]{2,0,1:T(2,128)} %copy.118), calls=%async_computation.4 | async-start | bytes 4194304 | tf_op jit(solution)/shard_map/all_to_all | solution.py:15
  390.8 7.6 %copy-start.22 = (s32[16]{0:T(128)S(1)}, s32[16]{0:T(128)}, u32[]{:S(2)}) copy-start(s32[16]{0:T(128)} %copy-done.21) | copy-start | bytes 196
  390.8 57.9 %all-to-all-start.10 = ((f32[2,512,1024]{2,0,1:T(2,128)}), f32[2,512,1024]{2,0,1:T(2,128)}, u32[]{:S(2)}, u32[]{:S(2)}) async-start(f32[2,512,1024]{2,0,1:T(2,128)} %copy.137), calls=%async_computation.10 | async-start | bytes 8388608 | tf_op jit(solution)/shard_map/all_to_all | solution.py:15
  398.6 2.3 copy-start.11
  398.6 2.3 copy-start.13
  448.6 20.8 %all-to-all-start.5 = ((f32[16,32,256]{2,0,1:T(8,128)}), f32[16,32,256]{2,0,1:T(8,128)S(1)}, u32[]{:S(2)}, u32[]{:S(2)}) async-start(f32[16,32,256]{2,0,1:T(8,128)} %copy.123), calls=%async_computation.5 | async-start | bytes 1048576 | tf_op jit(solution)/shard_map/all_to_all | solution.py:11
  457.7 78.1 %reduce-scatter.12.cloned.1.call-start = ((), (), s32[]{:S(2)}) async-start(), calls=%async_computation.18 | async-start | bytes 884736
  467.8 23.6 %copy-start.23 = (f32[256]{0:T(256)S(1)}, f32[256]{0:T(256)}, u32[]{:S(2)}) copy-start(f32[256]{0:T(256)} %param.11) | copy-start | bytes 3076
  469.4 22.0 %copy-start.4 = (f32[16,32,256]{2,0,1:T(8,128)}, f32[16,32,256]{2,0,1:T(8,128)S(1)}, u32[]{:S(2)}) copy-start(f32[16,32,256]{2,0,1:T(8,128)S(1)} %all-to-all-done.5) | copy-start | bytes 1572868
  469.4 22.0 %copy-start.5 = (f32[512,256]{1,0:T(8,128)S(1)}, f32[512,256]{1,0:T(8,128)}, u32[]{:S(2)}) copy-start(f32[512,256]{1,0:T(8,128)} %get-tuple-element.72) | copy-start | bytes 1572868
  491.4 3.2 copy-start.15
  494.9 42.8 %copy-start.3 = (f32[512,256]{1,0:T(8,128)S(1)}, f32[512,256]{1,0:T(8,128)}, u32[]{:S(2)}) copy-start(f32[512,256]{1,0:T(8,128)} %get-tuple-element.67) | copy-start | bytes 1572868
  496.1 42.7 %copy-start.24 = (u32[256]{0:T(256)S(1)}, u32[256]{0:T(256)}, u32[]{:S(2)}) copy-start(u32[256]{0:T(256)} %constant.108) | copy-start | bytes 3076
  496.1 43.9 %copy-start.20 = (f32[256]{0:T(256)S(1)}, f32[256]{0:T(256)}, u32[]{:S(2)}) copy-start(f32[256]{0:T(256)} %get-tuple-element.38) | copy-start | bytes 3076
  496.1 59.5 %copy-start.9 = (bf16[256,256]{1,0:T(8,128)(2,1)S(1)}, bf16[256,256]{1,0:T(8,128)(2,1)}, u32[]{:S(2)}) copy-start(bf16[256,256]{1,0:T(8,128)(2,1)} %param.9) | copy-start | bytes 393220
  496.2 77.9 %reduce-scatter.8.cloned.1.call-start = ((), (), s32[]{:S(2)}) async-start(), calls=%async_computation.16 | async-start | bytes 294912 | tf_op jit(solution)/shard_map/reduce_scatter | solution.py:161
  496.2 60.4 %copy-start.17 = (bf16[512,256]{1,0:T(8,128)(2,1)S(1)}, bf16[512,256]{1,0:T(8,128)(2,1)}, u32[]{:S(2)}) copy-start(bf16[512,256]{1,0:T(8,128)(2,1)} %copy-done.16) | copy-start | bytes 786436
  496.2 60.4 %copy-start.19 = (bf16[512,256]{1,0:T(8,128)(2,1)S(1)}, bf16[512,256]{1,0:T(8,128)(2,1)}, u32[]{:S(2)}) copy-start(bf16[512,256]{1,0:T(8,128)(2,1)} %copy-done.18) | copy-start | bytes 786436
  497.2 191.0 %all-reduce.4.cloned.1.call-start = ((), (), s32[]{:S(2)}) async-start(), calls=%async_computation.15 | async-start | bytes 786432 | tf_op jit(solution)/shard_map/psum | solution.py:158
  537.7 190.8 %reduce-scatter.10.cloned.1.call-start = ((), (), s32[]{:S(2)}) async-start(), calls=%async_computation.17 | async-start | bytes 589824
  (8 other events, 9.9 us)
Sparse Core Ops, SparseCore 0:
  496.3 39.5 reduce-scatter.11
  538.5 35.4 reduce-scatter.7
  577.2 110.8 all-reduce.3
  691.1 37.3 reduce-scatter.9
where the time goes:
time: 746 us; the launch traced here: 735 us
  waiting for transfers between devices  280 us (38%)
  blocking collectives  144 us (19%)
  matrix products  119 us (16%)
  starting transfers between devices  89.2 us (12%)
  local copies, waits for them, and re-layouts  69.3 us (9%)
  other arithmetic  18.7 us (3%)
  between operations  15.4 us (2%)
    psum x1, blocking collectives, shards(): in_sum, out_sum, skip_sum = lax.psum((in_term, out_term, skip_term), 'seq')  106 us
    all_to_all x4, waiting for transfers between devices, regroup_spectral(): lax.all_to_all(signal, 'seq', split_axis=1, concat_axis=0, tiled=True)  87.8 us
    unnamed x6, waiting for transfers between devices  77.2 us
    all_to_all x2, waiting for transfers between devices, forward_spectrum(): lax.all_to_all(spectrum, 'seq', split_axis=0, concat_axis=1, tiled=True)  39.1 us
    all_to_all x2, waiting for transfers between devices, inverse_field(): lax.all_to_all(spectrum, 'seq', split_axis=1, concat_axis=0, tiled=True)  38.6 us
    all_to_all x4, starting transfers between devices, regroup_spectral(): lax.all_to_all(signal, 'seq', split_axis=1, concat_axis=0, tiled=True)  33.9 us
    dot_general x2, matrix products, forward_spectrum(): jnp.einsum('kc,cjf->kjf', jnp.cos(inner_angle), spread, precision=HIGHEST)  30.2 us
    all_to_all x3, starting transfers between devices, regroup_real(): lax.all_to_all(signal, 'seq', split_axis=1, concat_axis=0, tiled=True)  23.2 us
  transfers between devices with their start and end apart: 15, of which 11 were waited for; matrix products, arithmetic and copies ran while one was open for 26% of the time, Pallas kernels for 0%

commit v1 on v0

--- a/solution.py
+++ b/solution.py
@@ -7,8 +7,15 @@
 HIGHEST = lax.Precision.HIGHEST
 
 
+def swap_blocks(array, axis, split, join):
+    n_dev = lax.axis_size(axis)
+    tiles = jnp.stack(jnp.split(array, n_dev, axis=split), axis=0)
+    tiles = lax.all_to_all(tiles, axis, split_axis=0, concat_axis=0)
+    return jnp.concatenate(tiles, axis=join)
+
+
 def regroup_real(signal):
-    return lax.all_to_all(signal, "seq", split_axis=1, concat_axis=0, tiled=True)
+    return swap_blocks(signal, "seq", 1, 0)
 
 
 def regroup_spectral(signal):

time: 746 us -> 807 us (1.082)
  local copies, waits for them, and re-layouts: 69.3 us -> 143 us
  blocking collectives: 144 us -> 122 us
  starting transfers between devices: 89.2 us -> 97.6 us
    unnamed x58 -> x194, local copies, waits for them, and re-layouts: 13.4 us -> 91.2 us
    all_to_all x1 -> x0, blocking collectives: 21.9 us -> none  [regroup_real(): lax.all_to_all(signal, 'seq', split_axis=1, concat_axis=0, tiled=True)]
    all_to_all x3 -> x4, starting transfers between devices: 23.2 us -> 31.8 us  [swap_blocks(): tiles = lax.all_to_all(tiles, axis, split_axis=0, concat_axis=0)]
    dot_general x2, matrix products: 30.2 us -> 21.8 us  [forward_spectrum(): jnp.einsum('kc,cjf->kjf', jnp.cos(inner_angle), spread, precision=HIGHEST)]
  transfers between devices with their start and end apart: 15 -> 16, of which waited for: 11 -> 11; matrix products, arithmetic and copies ran while one was open for 26% -> 29% of each run, Pallas kernels for 0% -> 0%
where the time goes in v1:
time: 807 us; the launch traced here: 797 us
  waiting for transfers between devices  276 us (34%)
  local copies, waits for them, and re-layouts  143 us (18%)
  matrix products  126 us (16%)
  blocking collectives  122 us (15%)
  starting transfers between devices  97.6 us (12%)
  other arithmetic  17.6 us (2%)
  between operations  15.4 us (2%)
    psum x1, blocking collectives, shards(): in_sum, out_sum, skip_sum = lax.psum((in_term, out_term, skip_term), 'seq')  106 us
    unnamed x194, local copies, waits for them, and re-layouts  91.2 us
    all_to_all x4, waiting for transfers between devices, regroup_spectral(): lax.all_to_all(signal, 'seq', split_axis=1, concat_axis=0, tiled=True)  83.3 us
    unnamed x6, waiting for transfers between devices  77.2 us
    all_to_all x2, waiting for transfers between devices, forward_spectrum(): lax.all_to_all(spectrum, 'seq', split_axis=0, concat_axis=1, tiled=True)  39.1 us
    all_to_all x2, waiting for transfers between devices, inverse_field(): lax.all_to_all(spectrum, 'seq', split_axis=1, concat_axis=0, tiled=True)  38.4 us
    all_to_all x4, starting transfers between devices, regroup_spectral(): lax.all_to_all(signal, 'seq', split_axis=1, concat_axis=0, tiled=True)  33.7 us
    all_to_all x4, starting transfers between devices, swap_blocks(): tiles = lax.all_to_all(tiles, axis, split_axis=0, concat_axis=0)  31.8 us
  transfers between devices with their start and end apart: 16, of which 11 were waited for; matrix products, arithmetic and copies ran while one was open for 29% of the time, Pallas kernels for 0%

profile of v1, /device:TPU:2, one launch (start us, length us, event | category | flops | bytes accessed | tf_op | source)
XLA Modules:
  0.0 797.3 jit_solution(7821003538712701303)
XLA Ops:
  31.5 7.6 all-to-all-start
  76.6 7.8 all-to-all-start.1
  90.4 44.1 %all-to-all-done.1 = f32[16,64,1024]{2,0,1:T(8,128)} async-done(((f32[16,64,1024]{2,0,1:T(8,128)}), f32[16,64,1024]{2,0,1:T(8,128)}, u32[]{:S(2)}, u32[]{:S(2)}) %all-to-all-start.1) | async-done | bytes 4194336 | tf_op jit(solution)/shard_map/all_to_all | solution.py:22
  134.5 9.1 %all-to-all-start.7 = ((f32[16,64,512]{2,0,1:T(8,128)}), f32[16,64,512]{2,0,1:T(8,128)}, u32[]{:S(2)}, u32[]{:S(2)}) async-start(f32[16,64,512]{2,0,1:T(8,128)} %copy.118), calls=%async_computation.7 | async-start | bytes 4194304 | tf_op jit(solution)/shard_map/all_to_all | solution.py:22
  146.1 10.9 %fusion.25 = f32[512,2,1024]{2,0,1:T(8,128)S(1)} fusion(f32[512,2,1024]{2,0,1:T(8,128)S(1)} %bitcast.657), kind=kOutput, calls=%fused_computation.52 | convolution fusion | flops 6446383104 | bytes 8388608 | tf_op jit(solution)/shard_map/kc,cjf->kjf/dot_general | solution.py:53
  157.0 11.2 %fusion.31 = f32[512,2,1024]{2,0,1:T(8,128)S(1)} fusion(f32[512,2,1024]{2,0,1:T(8,128)S(1)} %bitcast.658), kind=kOutput, calls=%fused_computation.58 | convolution fusion | flops 6446120960 | bytes 8388608 | tf_op jit(solution)/shard_map/kc,cjf->kjf/dot_general | solution.py:52
  175.1 7.4 all-to-all-start.2
  184.4 10.7 %fusion.23 = f32[512,2,512]{0,2,1:T(8,128)S(1)} fusion(f32[512,2,512]{2,0,1:T(8,128)S(1)} %bitcast.705), kind=kOutput, calls=%fused_computation.50 | convolution fusion | flops 3225157632 | bytes 4194304 | tf_op jit(solution)/shard_map/kc,cjf->kjf/dot_general | solution.py:53
  195.1 10.6 %fusion.28 = f32[512,2,512]{0,2,1:T(8,128)S(1)} fusion(f32[512,2,512]{2,0,1:T(8,128)S(1)} %bitcast.706), kind=kOutput, calls=%fused_computation.55 | convolution fusion | flops 3224895488 | bytes 4194304 | tf_op jit(solution)/shard_map/kc,cjf->kjf/dot_general | solution.py:52
  211.9 20.9 %all-to-all-done.2 = f32[512,2,1024]{2,1,0:T(2,128)} async-done(((f32[512,2,1024]{2,1,0:T(2,128)}), f32[512,2,1024]{2,1,0:T(2,128)}, u32[]{:S(2)}, u32[]{:S(2)}) %all-to-all-start.2) | async-done | bytes 4194336 | tf_op jit(solution)/shard_map/all_to_all | solution.py:61
  232.8 9.1 %all-to-all-start.8 = ((f32[512,2,512]{2,1,0:T(2,128)}), f32[512,2,512]{2,1,0:T(2,128)}, u32[]{:S(2)}, u32[]{:S(2)}) async-start(f32[512,2,512]{2,1,0:T(2,128)} %copy.122), calls=%async_computation.8 | async-start | bytes 4194304 | tf_op jit(solution)/shard_map/all_to_all | solution.py:61
  249.8 18.1 %all-to-all-done.8 = f32[512,2,512]{2,1,0:T(2,128)} async-done(((f32[512,2,512]{2,1,0:T(2,128)}), f32[512,2,512]{2,1,0:T(2,128)}, u32[]{:S(2)}, u32[]{:S(2)}) %all-to-all-start.8) | async-done | bytes 2097184 | tf_op jit(solution)/shard_map/all_to_all | solution.py:61
  268.0 7.6 all-to-all-start.3
  283.0 18.6 %all-to-all-done.3 = f32[16,64,512]{2,0,1:T(8,128)} async-done(((f32[16,64,512]{2,0,1:T(8,128)}), f32[16,64,512]{2,0,1:T(8,128)}, u32[]{:S(2)}, u32[]{:S(2)}) %all-to-all-start.3) | async-done | bytes 2097184 | tf_op jit(solution)/shard_map/all_to_all | solution.py:66
  301.5 7.7 all-to-all-start.9
  311.2 11.0 %convolution_bitcast_fusion.2 = f32[2,512,512]{1,2,0:T(8,128)S(1)} fusion(f32[512,2,512]{2,0,1:T(8,128)S(1)} %bitcast.707), kind=kOutput, calls=%fused_computation.22 | convolution fusion | flops 3224895488 | bytes 4194304 | tf_op jit(solution)/shard_map/kc,kjf->jcf/dot_general | solution.py:76
  322.2 11.0 %convolution_bitcast_fusion.3 = f32[2,512,512]{1,2,0:T(8,128)S(1)} fusion(f32[512,2,512]{2,0,1:T(8,128)S(1)} %bitcast.708), kind=kOutput, calls=%fused_computation.23 | convolution fusion | flops 3224895488 | bytes 4194304 | tf_op jit(solution)/shard_map/kc,kjf->jcf/dot_general | solution.py:75
  339.5 19.9 %all-to-all-done.9 = f32[16,64,1024]{2,0,1:T(8,128)} async-done(((f32[16,64,1024]{2,0,1:T(8,128)}), f32[16,64,1024]{2,0,1:T(8,128)}, u32[]{:S(2)}, u32[]{:S(2)}) %all-to-all-start.9) | async-done | bytes 4194336 | tf_op jit(solution)/shard_map/all_to_all | solution.py:66
  359.4 9.3 %all-to-all-start.4 = ((f32[2,512,512]{2,0,1:T(2,128)}), f32[2,512,512]{2,0,1:T(2,128)}, u32[]{:S(2)}, u32[]{:S(2)}) async-start(f32[2,512,512]{2,0,1:T(2,128)} %copy.111), calls=%async_computation.4 | async-start | bytes 4194304 | tf_op jit(solution)/shard_map/all_to_all | solution.py:22
  371.4 18.4 %convolution_bitcast_fusion = f32[2,512,1024]{1,2,0:T(8,128)} fusion(f32[512,2,1024]{2,0,1:T(8,128)S(1)} %bitcast.659), kind=kOutput, calls=%fused_computation.4 | convolution fusion | flops 6446120960 | bytes 8388608 | tf_op jit(solution)/shard_map/kc,kjf->jcf/dot_general | solution.py:76
  389.9 19.1 %convolution_bitcast_fusion.1 = f32[2,512,1024]{1,2,0:T(8,128)} fusion(f32[512,2,1024]{2,0,1:T(8,128)S(1)} %bitcast.660), kind=kOutput, calls=%fused_computation.5 | convolution fusion | flops 6446120960 | bytes 8388608 | tf_op jit(solution)/shard_map/kc,kjf->jcf/dot_general | solution.py:75
  433.7 7.4 all-to-all-start.10
  452.3 39.2 %all-to-all-done.10 = f32[2,512,1024]{2,0,1:T(2,128)} async-done(((f32[2,512,1024]{2,0,1:T(2,128)}), f32[2,512,1024]{2,0,1:T(2,128)}, u32[]{:S(2)}, u32[]{:S(2)}) %all-to-all-start.10) | async-done | bytes 4194336 | tf_op jit(solution)/shard_map/all_to_all | solution.py:22
  491.4 9.4 %all-to-all-start.5 = ((f32[32,16,1,256]{3,2,1,0:T(1,128)}), f32[32,16,1,256]{3,2,1,0:T(1,128)S(1)}, u32[]{:S(2)}, u32[]{:S(2)}) async-start(f32[32,16,1,256]{3,2,1,0:T(1,128)} %constant_dynamic-update-slice_fusion.32), calls=%async_computation.5 | async-start | bytes 1048576 | tf_op jit(solution)/shard_map/all_to_all | solution.py:13
  531.0 7.4 all-to-all-start.11
  539.4 13.6 %all-to-all-done.11 = f32[32,16,1,512]{3,2,1,0:T(1,128)} async-done(((f32[32,16,1,512]{3,2,1,0:T(1,128)}), f32[32,16,1,512]{3,2,1,0:T(1,128)}, u32[]{:S(2)}, u32[]{:S(2)}) %all-to-all-start.11) | async-done | bytes 1048608 | tf_op jit(solution)/shard_map/all_to_all | solution.py:13
  559.3 38.6 %reduce-scatter.12.cloned.1.call-done = f32[32,768]{1,0:T(8,128)} async-done(((f32[256,768]{1,0:T(8,128)}), f32[32,768]{1,0:T(8,128)}) %reduce-scatter.12.cloned.1.call-update) | async-done | bytes 98320
  602.2 15.5 %all-reduce = f32[256]{0:T(256)S(1)} all-reduce(f32[256]{0:T(256)S(1)} %broadcast_multiply_fusion), channel_id=5, replica_groups=mesh['dp'=8,'seq'=32] {'dp'}, use_global_device_ids=true, to_apply=%region_7.8.clone | all-reduce | flops 256 | bytes 2048
  619.8 16.2 %reduce-scatter.8.cloned.1.call-done = f32[32,256]{1,0:T(8,128)} async-done(((f32[256,256]{1,0:T(8,128)}), f32[32,256]{1,0:T(8,128)}) %reduce-scatter.8.cloned.1.call-update) | async-done | bytes 32784 | tf_op jit(solution)/shard_map/reduce_scatter | solution.py:168
  636.0 106.2 %all-reduce.1 = (f32[32,256]{1,0:T(8,128)}, f32[32]{0:T(128)}) all-reduce(f32[32,256]{1,0:T(8,128)} %reduce-scatter.8.cloned.1.call-done, f32[32]{0:T(128)S(1)} %dynamic-slice.1), channel_id=1, replica_groups=mesh['dp'=8,'seq'=32] {'seq'}, use_global_device_ids=true, to_apply=%region_2.3 | all-reduce | flops 8224 | bytes 65792 | tf_op jit(solution)/shard_map/psum | solution.py:165
  742.2 8.1 %all-reduce.4.cloned.1.call-done = f32[32,768]{0,1:T(8,128)} async-done(((f32[32,768]{0,1:T(8,128)}), f32[32,768]{0,1:T(8,128)}) %all-reduce.4.cloned.1.call-update) | async-done | bytes 98320 | tf_op jit(solution)/shard_map/psum | solution.py:165
  752.0 38.5 %reduce-scatter.10.cloned.1.call-done = f32[32,512]{1,0:T(8,128)} async-done(((f32[256,512]{1,0:T(8,128)}), f32[32,512]{1,0:T(8,128)}) %reduce-scatter.10.cloned.1.call-update) | async-done | bytes 65552
  (266 shorter events, 191.5 us)
Async XLA Ops:
  11.1 46.7 %copy-start.7 = (f32[512,256]{1,0:T(8,128)}, f32[512,256]{1,0:T(8,128)S(1)}, u32[]{:S(2)}) copy-start(f32[512,256]{1,0:T(8,128)S(1)} %get-tuple-element.39) | copy-start | bytes 1572868
  31.5 27.0 %all-to-all-start = ((f32[32,1,16,512]{3,2,1,0:T(8,128)}), f32[32,1,16,512]{3,2,1,0:T(8,128)S(1)}, u32[]{:S(2)}, u32[]{:S(2)}) async-start(f32[32,1,16,512]{3,2,1,0:T(8,128)} %constant_dynamic-update-slice_fusion), calls=%async_computation | async-start | bytes 2097152 | tf_op jit(solution)/shard_map/all_to_all | solution.py:13
  39.1 18.8 %copy-start.27 = (s32[16]{0:T(128)}, s32[16]{0:T(128)S(1)}, u32[]{:S(2)}) copy-start(s32[16]{0:T(128)S(1)} %iota_add_fusion) | copy-start | bytes 196
  58.5 18.1 %all-to-all-start.6 = ((f32[32,1,16,256]{3,2,1,0:T(8,128)}), f32[32,1,16,256]{3,2,1,0:T(8,128)S(1)}, u32[]{:S(2)}, u32[]{:S(2)}) async-start(f32[32,1,16,256]{3,2,1,0:T(8,128)} %constant_dynamic-update-slice_fusion.64), calls=%async_computation.6 | async-start | bytes 1048576 | tf_op jit(solution)/shard_map/all_to_all | solution.py:13
  76.6 57.9 %all-to-all-start.1 = ((f32[16,64,1024]{2,0,1:T(8,128)}), f32[16,64,1024]{2,0,1:T(8,128)}, u32[]{:S(2)}, u32[]{:S(2)}) async-start(f32[16,64,1024]{2,0,1:T(8,128)} %copy.103), calls=%async_computation.1 | async-start | bytes 8388608 | tf_op jit(solution)/shard_map/all_to_all | solution.py:22
  134.5 40.6 %all-to-all-start.7 = ((f32[16,64,512]{2,0,1:T(8,128)}), f32[16,64,512]{2,0,1:T(8,128)}, u32[]{:S(2)}, u32[]{:S(2)}) async-start(f32[16,64,512]{2,0,1:T(8,128)} %copy.118), calls=%async_computation.7 | async-start | bytes 4194304 | tf_op jit(solution)/shard_map/all_to_all | solution.py:22
  175.1 57.7 %all-to-all-start.2 = ((f32[512,2,1024]{2,1,0:T(2,128)}), f32[512,2,1024]{2,1,0:T(2,128)}, u32[]{:S(2)}, u32[]{:S(2)}) async-start(f32[512,2,1024]{2,1,0:T(2,128)} %copy.105), calls=%async_computation.2 | async-start | bytes 8388608 | tf_op jit(solution)/shard_map/all_to_all | solution.py:61
  232.8 35.1 %all-to-all-start.8 = ((f32[512,2,512]{2,1,0:T(2,128)}), f32[512,2,512]{2,1,0:T(2,128)}, u32[]{:S(2)}, u32[]{:S(2)}) async-start(f32[512,2,512]{2,1,0:T(2,128)} %copy.122), calls=%async_computation.8 | async-start | bytes 4194304 | tf_op jit(solution)/shard_map/all_to_all | solution.py:61
  268.0 33.6 %all-to-all-start.3 = ((f32[16,64,512]{2,0,1:T(8,128)}), f32[16,64,512]{2,0,1:T(8,128)}, u32[]{:S(2)}, u32[]{:S(2)}) async-start(f32[16,64,512]{2,0,1:T(8,128)} %pad_maximum_fusion.4), calls=%async_computation.3 | async-start | bytes 4194304 | tf_op jit(solution)/shard_map/all_to_all | solution.py:66
  301.5 57.9 %all-to-all-start.9 = ((f32[16,64,1024]{2,0,1:T(8,128)}), f32[16,64,1024]{2,0,1:T(8,128)}, u32[]{:S(2)}, u32[]{:S(2)}) async-start(f32[16,64,1024]{2,0,1:T(8,128)} %pad_maximum_fusion.2), calls=%async_computation.9 | async-start | bytes 8388608 | tf_op jit(solution)/shard_map/all_to_all | solution.py:66
  339.5 29.2 %copy-start.28 = (s32[16]{0:T(128)S(1)}, s32[16]{0:T(128)}, u32[]{:S(2)}) copy-start(s32[16]{0:T(128)} %copy-done.27) | copy-start | bytes 196
  359.4 49.5 %all-to-all-start.4 = ((f32[2,512,512]{2,0,1:T(2,128)}), f32[2,512,512]{2,0,1:T(2,128)}, u32[]{:S(2)}, u32[]{:S(2)}) async-start(f32[2,512,512]{2,0,1:T(2,128)} %copy.111), calls=%async_computation.4 | async-start | bytes 4194304 | tf_op jit(solution)/shard_map/all_to_all | solution.py:22
  368.9 42.4 %copy-start.17 = (f32[64,16]{1,0:T(8,128)}, f32[64,16]{1,0:T(8,128)S(1)}, u32[]{:S(2)}) copy-start(f32[64,16]{1,0:T(8,128)S(1)} %get-tuple-element.68) | copy-start | bytes 12292
  368.9 42.4 %copy-start.19 = (f32[64,16]{1,0:T(8,128)}, f32[64,16]{1,0:T(8,128)S(1)}, u32[]{:S(2)}) copy-start(f32[64,16]{1,0:T(8,128)S(1)} %get-tuple-element.69) | copy-start | bytes 12292
  411.3 11.6 %copy-start.3 = (f32[2,512,1024]{1,2,0:T(8,128)S(1)}, f32[2,512,1024]{1,2,0:T(8,128)}, u32[]{:S(2)}) copy-start(f32[2,512,1024]{1,2,0:T(8,128)} %convolution_bitcast_fusion) | copy-start | bytes 12582916
  411.3 11.6 %copy-start.4 = (f32[2,512,1024]{1,2,0:T(8,128)S(1)}, f32[2,512,1024]{1,2,0:T(8,128)}, u32[]{:S(2)}) copy-start(f32[2,512,1024]{1,2,0:T(8,128)} %convolution_bitcast_fusion.1) | copy-start | bytes 12582916
  433.7 57.7 %all-to-all-start.10 = ((f32[2,512,1024]{2,0,1:T(2,128)}), f32[2,512,1024]{2,0,1:T(2,128)}, u32[]{:S(2)}, u32[]{:S(2)}) async-start(f32[2,512,1024]{2,0,1:T(2,128)} %copy.128), calls=%async_computation.10 | async-start | bytes 8388608 | tf_op jit(solution)/shard_map/all_to_all | solution.py:22
  491.4 39.6 %all-to-all-start.5 = ((f32[32,16,1,256]{3,2,1,0:T(1,128)}), f32[32,16,1,256]{3,2,1,0:T(1,128)S(1)}, u32[]{:S(2)}, u32[]{:S(2)}) async-start(f32[32,16,1,256]{3,2,1,0:T(1,128)} %constant_dynamic-update-slice_fusion.32), calls=%async_computation.5 | async-start | bytes 1048576 | tf_op jit(solution)/shard_map/all_to_all | solution.py:13
  531.0 21.9 %all-to-all-start.11 = ((f32[32,16,1,512]{3,2,1,0:T(1,128)}), f32[32,16,1,512]{3,2,1,0:T(1,128)}, u32[]{:S(2)}, u32[]{:S(2)}) async-start(f32[32,16,1,512]{3,2,1,0:T(1,128)} %constant_dynamic-update-slice_fusion.96), calls=%async_computation.11 | async-start | bytes 2097152 | tf_op jit(solution)/shard_map/all_to_all | solution.py:13
  538.5 15.9 %copy-start.6 = (f32[512,256]{1,0:T(8,128)S(1)}, f32[512,256]{1,0:T(8,128)}, u32[]{:S(2)}) copy-start(f32[512,256]{1,0:T(8,128)} %copy-done.5) | copy-start | bytes 1572868
  538.5 15.9 %copy-start.8 = (f32[512,256]{1,0:T(8,128)S(1)}, f32[512,256]{1,0:T(8,128)}, u32[]{:S(2)}) copy-start(f32[512,256]{1,0:T(8,128)} %copy-done.7) | copy-start | bytes 1572868
  538.5 15.9 %copy-start.29 = (f32[256]{0:T(256)S(1)}, f32[256]{0:T(256)}, u32[]{:S(2)}) copy-start(f32[256]{0:T(256)} %param.11) | copy-start | bytes 3076
  538.5 59.5 %reduce-scatter.12.cloned.1.call-start = ((), (), s32[]{:S(2)}) async-start(), calls=%async_computation.18 | async-start | bytes 884736
  557.0 42.9 %copy-start.9 = (f32[512,256]{1,0:T(8,128)S(1)}, f32[512,256]{1,0:T(8,128)}, u32[]{:S(2)}) copy-start(f32[512,256]{1,0:T(8,128)} %get-tuple-element.67) | copy-start | bytes 1572868
  558.2 42.7 %copy-start.30 = (u32[256]{0:T(256)S(1)}, u32[256]{0:T(256)}, u32[]{:S(2)}) copy-start(u32[256]{0:T(256)} %constant.108) | copy-start | bytes 3076
  558.2 44.0 %copy-start.26 = (f32[256]{0:T(256)S(1)}, f32[256]{0:T(256)}, u32[]{:S(2)}) copy-start(f32[256]{0:T(256)} %get-tuple-element.38) | copy-start | bytes 3076
  558.2 59.6 %copy-start.15 = (bf16[256,256]{1,0:T(8,128)(2,1)S(1)}, bf16[256,256]{1,0:T(8,128)(2,1)}, u32[]{:S(2)}) copy-start(bf16[256,256]{1,0:T(8,128)(2,1)} %param.9) | copy-start | bytes 393220
  558.2 77.8 %reduce-scatter.8.cloned.1.call-start = ((), (), s32[]{:S(2)}) async-start(), calls=%async_computation.16 | async-start | bytes 294912 | tf_op jit(solution)/shard_map/reduce_scatter | solution.py:168
  558.3 60.4 %copy-start.23 = (bf16[512,256]{1,0:T(8,128)(2,1)S(1)}, bf16[512,256]{1,0:T(8,128)(2,1)}, u32[]{:S(2)}) copy-start(bf16[512,256]{1,0:T(8,128)(2,1)} %copy-done.22) | copy-start | bytes 786436
  558.3 60.4 %copy-start.25 = (bf16[512,256]{1,0:T(8,128)(2,1)S(1)}, bf16[512,256]{1,0:T(8,128)(2,1)}, u32[]{:S(2)}) copy-start(bf16[512,256]{1,0:T(8,128)(2,1)} %copy-done.24) | copy-start | bytes 786436
  559.3 191.0 %all-reduce.4.cloned.1.call-start = ((), (), s32[]{:S(2)}) async-start(), calls=%async_computation.15 | async-start | bytes 786432 | tf_op jit(solution)/shard_map/psum | solution.py:165
  599.8 190.7 %reduce-scatter.10.cloned.1.call-start = ((), (), s32[]{:S(2)}) async-start(), calls=%async_computation.17 | async-start | bytes 589824
  (15 other events, 25.2 us)
Sparse Core Ops, SparseCore 0:
  558.3 39.6 reduce-scatter.11
  600.6 35.3 reduce-scatter.7
  639.2 110.9 all-reduce.3
  753.2 37.3 reduce-scatter.9
